TPU v7x, 128 devices: a whole 4x4x4 slice. The times are simulated.
128 devices in a mesh: ctx: 32 (over x_hi, z, y), tp: 4 (over x_lo, core).
Axes of the slice: x: 4 (x_hi: 2, x_lo: 2; x = x_hi * 2 + x_lo), y: 4, z: 4, core: 2. Of those that a mesh axis runs over, the one named last changes fastest.
Arguments:
- qkv: bfloat16 [3, 8192, 4096], P(None, 'ctx', 'tp'), may hold values from -6 to 6
- filters: bfloat16 [256, 128], P('tp'), may hold values from -0.5 to 0.5
- w_out: bfloat16 [4096, 4096], P(None, 'tp'), may hold values from -0.09375 to 0.09375
- cotangent: bfloat16 [8192, 4096], P(('ctx', 'tp')), may hold values from -24 to 24
- doc_lens: int32 [64], replicated, may hold values from 1 to 384, 8192 in all
Outputs:
- grad_qkv: bfloat16 [3, 8192, 4096], P(None, 'ctx', 'tp')
- grad_filters: float32 [256, 128], P('tp')
- grad_w_out: float32 [4096, 4096], P('ctx', 'tp')
All inputs are finite; a program needn't handle non-finite values.
Results may differ from a plain program's by a relative error of at most 0.005.
Values may be sent and summed in bfloat16 or wider, within the bound.
A program may use at most 128 MiB of HBM per device.

v0:
```python
import math

import jax
import jax.numpy as jnp
from jax import lax
from jax.sharding import PartitionSpec as P


def extended_2(cells, sides, width):
    for axis, dim in sides:
        count = lax.axis_size(axis)
        ends = count - 1
        head = lax.slice_in_dim(cells, 0, width, axis=dim)
        tail = lax.slice_in_dim(cells, cells.shape[dim] - width, cells.shape[dim], axis=dim)
        cells = jnp.concatenate(
            [
                lax.ppermute(tail, axis, [(i, (i + 1) % count) for i in range(ends)]),
                cells,
                lax.ppermute(head, axis, [((i + 1) % count, i) for i in range(ends)]),
            ],
            axis=dim,
        )
    return cells


def banded(filters):
    groups, tap_count = filters.shape
    width = 2 * tap_count
    blank = jnp.zeros((groups, 1), filters.dtype)
    tailing = jnp.zeros((groups, width - tap_count), filters.dtype)
    pattern = jnp.concatenate([blank, jnp.flip(filters, axis=1), tailing], axis=1)
    tiled = jnp.broadcast_to(pattern[:, None, :], (groups, tap_count, width + 1)).reshape(
        groups, tap_count * (width + 1)
    )
    return tiled[:, : tap_count * width].reshape(groups, tap_count, width)


def diagonals(products):
    groups, tap_count, width = products.shape
    flattened = jnp.pad(products.reshape(groups, tap_count * width), ((0, 0), (0, tap_count)))
    sheared = flattened.reshape(groups, tap_count, width + 1)[:, :, 1 : tap_count + 1]
    return jnp.flip(jnp.sum(sheared, axis=1), axis=1)


def doc_reach(positions, doc_lens):
    starts = jnp.cumsum(doc_lens) - doc_lens
    below = jnp.where(starts[None, :] <= positions[:, None], starts[None, :], 0)
    return positions - jnp.max(below, axis=1)


def band_mask(doc_offset, tap_count):
    row_ids = lax.broadcasted_iota(jnp.int32, (tap_count, 2 * tap_count), 0)
    col_ids = lax.broadcasted_iota(jnp.int32, (tap_count, 2 * tap_count), 1)
    return (row_ids - col_ids + tap_count <= doc_offset[:, None]).astype(jnp.float32)


def spread_back(kernel, rows_grad, groups_local, group_width):
    tap_count = rows_grad.shape[0]
    grad_f = rows_grad.astype(jnp.float32).reshape(tap_count, groups_local, group_width)
    spread = jnp.einsum("gij,igc->jgc", kernel, grad_f, precision=lax.Precision.HIGHEST)
    return spread.reshape(2 * tap_count, groups_local * group_width)


def local(qkv, filters, w_out, cotangent, doc_lens):
    queries, key_in, values = (qkv[0], qkv[1], qkv[2])
    tok_ctx, width_local = queries.shape
    span_rows = tok_ctx // 2
    groups_local, tap_count = filters.shape
    group_width = width_local // groups_local
    blocks = span_rows // tap_count
    n_ctx = lax.axis_size("ctx")
    ctx_rank = lax.axis_index("ctx")
    tokens = tok_ctx * n_ctx
    last_rank = ctx_rank == n_ctx - 1
    exact = lax.Precision.HIGHEST
    offsets = jnp.arange(span_rows, dtype=jnp.int32)
    first_pos = ctx_rank * span_rows + offsets
    second_pos = (2 * n_ctx - 1 - ctx_rank) * span_rows + offsets
    doc_offset = jnp.stack([doc_reach(first_pos, doc_lens), doc_reach(second_pos, doc_lens)])
    hidden = (key_in.astype(jnp.float32) * values.astype(jnp.float32)).astype(jnp.bfloat16)
    hidden = hidden.reshape(2, span_rows, width_local)
    outgoing = jnp.concatenate([hidden[1], hidden[0]], axis=0)
    padded = extended_2(outgoing, (("ctx", 0),), tap_count)
    tail_first = padded[:tap_count]
    tail_second = jnp.where(last_rank, hidden[0], padded[3 * tap_count :])
    extended = jnp.concatenate([jnp.stack([tail_first, tail_second]), hidden], axis=1)
    full_cot = lax.all_gather(cotangent, "tp", axis=0, tiled=True)
    grad_y = jnp.dot(full_cot, w_out, preferred_element_type=jnp.float32)
    grad_c = (
        (queries.astype(jnp.float32) * grad_y)
        .astype(jnp.bfloat16)
        .reshape(2, span_rows, width_local)
    )
    kernel_base = banded(filters.astype(jnp.float32))

    def advance(total, block_index):
        which_slot = block_index // blocks
        within = block_index % blocks * tap_count
        window = lax.dynamic_slice(
            extended, (which_slot, within, 0), (1, 2 * tap_count, width_local)
        )[0]
        rows_grad = lax.dynamic_slice(grad_c, (which_slot, within, 0), (1, tap_count, width_local))[
            0
        ]
        rows_offset = lax.dynamic_slice(doc_offset, (which_slot, within), (1, tap_count))[0]
        keep = band_mask(rows_offset, tap_count)
        kernel = kernel_base * keep[None]
        window_f = window.astype(jnp.float32).reshape(2 * tap_count, groups_local, group_width)
        grad_f = rows_grad.astype(jnp.float32).reshape(tap_count, groups_local, group_width)
        conv_rows = jnp.einsum("gij,jgc->igc", kernel, window_f, precision=exact).reshape(
            tap_count, width_local
        )
        spread = jnp.einsum("gij,igc->jgc", kernel, grad_f, precision=exact).reshape(
            2 * tap_count, width_local
        )
        products = jnp.einsum("igc,jgc->gij", grad_f, window_f, precision=exact)
        total = total + diagonals(products * keep[None])
        return (total, (conv_rows, spread[:tap_count], spread[tap_count:]))

    filter_total, (conv_blocks, spill_rows, own_rows) = lax.scan(
        advance,
        jnp.zeros((groups_local, tap_count), jnp.float32),
        jnp.arange(2 * blocks, dtype=jnp.int32),
    )
    conv_out = conv_blocks.reshape(tok_ctx, width_local)
    spill_rows = spill_rows.reshape(2, blocks, tap_count, width_local)
    own_rows = own_rows.reshape(2, blocks, tap_count, width_local)
    head_rows = jnp.concatenate([grad_c[0, :tap_count], grad_c[1, :tap_count]], axis=0)
    received = extended_2(head_rows, (("ctx", 0),), tap_count)
    head_first = jnp.where(last_rank, grad_c[1, :tap_count], received[3 * tap_count :])
    head_second = received[:tap_count]
    tap_ids = jnp.arange(tap_count, dtype=jnp.int32)
    next_first = (ctx_rank + 1) * span_rows + tap_ids
    next_second = (2 * n_ctx - ctx_rank) * span_rows + tap_ids

    def pull_back(head_grad, head_pos):
        kernel = kernel_base * band_mask(doc_reach(head_pos, doc_lens), tap_count)[None]
        return spread_back(kernel, head_grad, groups_local, group_width)[:tap_count]

    spill_first = pull_back(head_first, next_first)
    spill_second = pull_back(head_second, next_second)
    following = jnp.concatenate(
        [spill_rows[:, 1:], jnp.stack([spill_first, spill_second])[:, None]], axis=1
    )
    grad_h = (own_rows + following).reshape(tok_ctx, width_local)
    grad_q = (grad_y * conv_out).astype(jnp.bfloat16)
    grad_k = (grad_h * values.astype(jnp.float32)).astype(jnp.bfloat16)
    grad_v = (grad_h * key_in.astype(jnp.float32)).astype(jnp.bfloat16)
    grad_qkv = jnp.stack([grad_q, grad_k, grad_v])
    grad_scale = 1.0 / math.sqrt(tokens)
    grad_filters = lax.psum(filter_total, "ctx") * grad_scale
    gated = (queries.astype(jnp.float32) * conv_out).astype(jnp.bfloat16)
    grad_w = lax.psum_scatter(
        lax.dot_general(
            full_cot, gated, (((0,), (0,)), ((), ())), preferred_element_type=jnp.float32
        ),
        "ctx",
        scatter_dimension=0,
        tiled=True,
    )
    return (grad_qkv, grad_filters, grad_w * grad_scale)


def solution(mesh):
    return jax.shard_map(
        local,
        mesh=mesh,
        in_specs=(P(None, "ctx", "tp"), P("tp", None), P(None, "tp"), P(("ctx", "tp"), None), P()),
        out_specs=(P(None, "ctx", "tp"), P("tp", None), P("ctx", "tp")),
        check_vma=False,
    )
```

profile of v0, /device:TPU:4, one launch (start us, length us, event | category | flops | bytes accessed | tf_op | source)
XLA Modules:
  0.0 395.9 jit_solution(11501874476775541881)
XLA Ops:
  7.9 1.4 fusion.24
  9.4 3.5 collective-permute-start
  12.9 8.1 %collective-permute-start.1 = (bf16[128,1024]{1,0:T(8,128)(2,1)S(1)}, bf16[128,1024]{1,0:T(8,128)(2,1)S(1)}, u32[]{:S(2)}, u32[]{:S(2)}) collective-permute-start(bf16[128,1024]{1,0:T(8,128)(2,1)S(1)} %get-tuple-element.242), channel_id=1, source_target_pairs={{4,0},{8,4},{12,8},{16,12},{20,16},{24,20},{28,24},{32,28},{36,32}... | collective-permute-start | bytes 786440 | tf_op jit(solution)/shard_map/ppermute | solution.py:19
  24.3 5.4 %broadcast_in_dim.69 = f32[64,128,257]{2,1,0:T(8,128)} broadcast(f32[64,257]{1,0:T(8,128)S(1)} %maximum_maximum_fusion), dimensions={0,2} | broadcast | bytes 8487168 | tf_op jit(solution)/shard_map/broadcast_in_dim | solution.py:32
  29.6 12.3 %reshape.244 = f32[64,32896]{1,0:T(8,128)} reshape(f32[64,128,257]{2,1,0:T(8,128)} %broadcast_in_dim.69) | data formatting | bytes 16842752 | tf_op jit(solution)/shard_map/reshape | solution.py:32
  41.9 3.4 slice-done
  45.3 5.8 %copy.37 = f32[8,8,128,256]{3,2,1,0:T(8,128)} copy(f32[8,8,128,256]{3,1,2,0:T(8,128)S(1)} %bitcast.101) | data formatting | bytes 16777216
  51.2 7.4 %fusion.26 = (bf16[256,1024]{1,0:T(8,128)(2,1)S(1)}, f32[256,1024]{1,0:T(8,128)}) fusion(bf16[3,256,1024]{2,1,0:T(8,128)(2,1)} %param.7, bf16[256,4096]{1,0:T(8,128)(2,1)} %all-gather.2.cloned.1.call-done, bf16[4096,1024]{1,0:T(8,128)(2,1)} %param.9), kind=kOutput, calls=%fused_computation.36 | convolution fusion | flops 2148270080 | bytes 12582912 | tf_op jit(solution)/shard_map/dot_general | solution.py:88
  58.6 90.4 %while.19 = (s32[]{:T(128)}, f32[64,128]{1,0:T(8,128)}, f32[2,128,1024]{2,1,0:T(8,128)}, f32[2,128,1024]{1,2,0:T(8,128)}, s32[2]{0:T(128)S(1)}, /*index=5*/bf16[...) while((s32[]{:T(128)}, f32[64,128]{1,0:T(8,128)}, ...), condition=%wide.region_5.6_spmd.clone, body=%wide.region_3.5_spmd.clone.sunk | while | flops 879894528 | bytes 99649336 | solution.py:120
  61.6 6.4 %fusion.63 = f32[64,16,128]{2,1,0:T(8,128)S(1)} fusion(bf16[256,64,16]{0,2,1:T(8,128)(2,1)S(1)} %bitcast.95, f32[64,128,256]{2,1,0:T(8,128)} %get-tuple-element.336, f32[128,256]{1,0:T(8,128)S(1)} %fusion.62), kind=kOutput, calls=%fused_computation.2.clone.1 | convolution fusion | flops 404750336 | bytes 9568256 | tf_op jit(solution)/shard_map/while/body/eval_jaxpr/gij,jgc->igc/dot_general | solution.py:110
  69.1 5.4 %fusion.64 = f32[256,64,16]{0,2,1:T(8,128)S(1)} fusion(bf16[128,64,16]{0,2,1:T(8,128)(2,1)S(1)} %bitcast.97, f32[64,128,256]{2,1,0:T(8,128)} %get-tuple-element.336, f32[128,256]{1,0:T(8,128)S(1)} %fusion.62), kind=kOutput, calls=%fused_computation.8.clone.1 | convolution fusion | flops 404750336 | bytes 9830400 | tf_op jit(solution)/shard_map/while/body/eval_jaxpr/gij,igc->jgc/dot_general | solution.py:113
  75.9 4.7 %copy.44 = f32[8,8,128,256]{3,1,2,0:T(8,128)S(1)} copy(f32[8,8,128,256]{3,2,1,0:T(8,128)S(1)} %bitcast.93) | data formatting | bytes 16777216 | tf_op jit(solution)/shard_map/while
  80.6 3.8 pad.34
  84.4 14.2 %reshape.258 = f32[64,128,257]{2,1,0:T(8,128)} reshape(f32[64,32896]{1,0:T(8,128)} %pad.34) | data formatting | bytes 16842752 | tf_op jit(solution)/shard_map/while/body/eval_jaxpr/reshape | solution.py:41
  98.6 4.5 %slice_reduce_fusion.2 = f32[64,128]{1,0:T(8,128)S(1)} fusion(f32[64,128,257]{2,1,0:T(8,128)} %reshape.258), kind=kLoop, calls=%fused_computation.4.clone.1 | loop fusion | flops 1040384 | bytes 4227072 | tf_op jit(solution)/shard_map/while/body/eval_jaxpr/reduce_sum | solution.py:42
  106.8 6.4 %fusion.63 = f32[64,16,128]{2,1,0:T(8,128)S(1)} fusion(bf16[256,64,16]{0,2,1:T(8,128)(2,1)S(1)} %bitcast.95, f32[64,128,256]{2,1,0:T(8,128)} %get-tuple-element.336, f32[128,256]{1,0:T(8,128)S(1)} %fusion.62), kind=kOutput, calls=%fused_computation.2.clone.1 | convolution fusion | flops 404750336 | bytes 9568256 | tf_op jit(solution)/shard_map/while/body/eval_jaxpr/gij,jgc->igc/dot_general | solution.py:110
  114.3 5.4 %fusion.64 = f32[256,64,16]{0,2,1:T(8,128)S(1)} fusion(bf16[128,64,16]{0,2,1:T(8,128)(2,1)S(1)} %bitcast.97, f32[64,128,256]{2,1,0:T(8,128)} %get-tuple-element.336, f32[128,256]{1,0:T(8,128)S(1)} %fusion.62), kind=kOutput, calls=%fused_computation.8.clone.1 | convolution fusion | flops 404750336 | bytes 9830400 | tf_op jit(solution)/shard_map/while/body/eval_jaxpr/gij,igc->jgc/dot_general | solution.py:113
  121.1 4.7 %copy.44 = f32[8,8,128,256]{3,1,2,0:T(8,128)S(1)} copy(f32[8,8,128,256]{3,2,1,0:T(8,128)S(1)} %bitcast.93) | data formatting | bytes 16777216 | tf_op jit(solution)/shard_map/while
  125.9 3.8 pad.34
  129.6 14.2 %reshape.258 = f32[64,128,257]{2,1,0:T(8,128)} reshape(f32[64,32896]{1,0:T(8,128)} %pad.34) | data formatting | bytes 16842752 | tf_op jit(solution)/shard_map/while/body/eval_jaxpr/reshape | solution.py:41
  143.8 4.5 %slice_reduce_fusion.2 = f32[64,128]{1,0:T(8,128)S(1)} fusion(f32[64,128,257]{2,1,0:T(8,128)} %reshape.258), kind=kLoop, calls=%fused_computation.4.clone.1 | loop fusion | flops 1040384 | bytes 4227072 | tf_op jit(solution)/shard_map/while/body/eval_jaxpr/reduce_sum | solution.py:42
  149.0 2.8 fusion.27
  151.8 9.7 %convolution_bitcast_fusion = f32[4096,1024]{0,1:T(8,128)} fusion(bf16[256,1024]{1,0:T(8,128)(2,1)S(1)} %get-tuple-element.237, bf16[256,4096]{1,0:T(8,128)(2,1)} %all-gather.2.cloned.1.call-done), kind=kOutput, calls=%fused_computation.18 | convolution fusion | flops 2147483648 | bytes 19398656 | tf_op jit(solution)/shard_map/dot_general | solution.py:154
  162.3 2.8 collective-permute-start.2
  165.2 184.5 %psum.7 = f32[64,128]{1,0:T(8,128)S(1)} all-reduce(f32[64,128]{1,0:T(8,128)S(1)} %copy-done.5), channel_id=1, replica_groups=mesh['ctx'=32,'tp'=4] {'ctx'}, use_global_device_ids=true, to_apply=%region_8.9 | all-reduce | flops 8192 | bytes 65536 | tf_op jit(solution)/shard_map/psum | solution.py:151
  350.5 1.9 collective-permute-start.3
  352.4 5.4 %fusion.17 = f32[256,64,16]{0,2,1:T(8,128)S(1)} fusion(bf16[128,64,16]{0,2,1:T(8,128)(2,1)S(1)} %bitcast.110, f32[64,128,256]{2,1,0:T(8,128)} %get-tuple-element.343, f32[128,256]{1,0:T(8,128)S(1)} %fusion.31), kind=kOutput, calls=%fused_computation.26 | convolution fusion | flops 404750336 | bytes 9830400 | tf_op jit(solution)/shard_map/gij,igc->jgc/dot_general | solution.py:60
  358.7 10.9 %collective-permute-done.3 = bf16[128,1024]{1,0:T(8,128)(2,1)S(1)} collective-permute-done((bf16[128,1024]{1,0:T(8,128)(2,1)S(1)}, bf16[128,1024]{1,0:T(8,128)(2,1)S(1)}, u32[]{:S(2)}, u32[]{:S(2)}) %collective-permute-start.3) | collective-permute-done | bytes 262176 | tf_op jit(solution)/shard_map/ppermute | solution.py:17
  369.8 5.6 %fusion.20 = f32[256,64,16]{0,2,1:T(8,128)S(1)} fusion(bf16[128,64,16]{0,2,1:T(8,128)(2,1)S(1)} %bitcast.111, f32[64,128,256]{2,1,0:T(8,128)} %get-tuple-element.343, f32[128,256]{1,0:T(8,128)S(1)} %fusion.32), kind=kOutput, calls=%fused_computation.27 | convolution fusion | flops 404750336 | bytes 9830400 | tf_op jit(solution)/shard_map/gij,igc->jgc/dot_general | solution.py:60
  375.4 1.4 maximum_add_fusion
  378.1 1.5 fusion.25
  380.9 6.1 %reduce-scatter.2.cloned.1.call-done = f32[128,1024]{0,1:T(8,128)} async-done(((f32[4096,1024]{0,1:T(8,128)}), f32[128,1024]{0,1:T(8,128)}) %reduce-scatter.2.cloned.1.call-update) | async-done | bytes 524304 | tf_op jit(solution)/shard_map/reduce_scatter | solution.py:153
  (103 shorter events, 20.0 us)
Async XLA Ops:
  7.2 44.1 %all-gather.2.cloned.1.call-start = ((), (), s32[]{:S(2)}) async-start(), calls=%async_computation.1 | async-start | bytes 2621440 | tf_op jit(solution)/shard_map/all_gather | solution.py:87
  7.9 379.1 %reduce-scatter.2.cloned.1.call-start = ((), (), s32[]{:S(2)}) async-start(), calls=%async_computation.2 | async-start | bytes 17301504 | tf_op jit(solution)/shard_map/reduce_scatter | solution.py:153
  9.4 41.7 %collective-permute-start = (bf16[128,1024]{1,0:T(8,128)(2,1)S(1)}, bf16[128,1024]{1,0:T(8,128)(2,1)S(1)}, u32[]{:S(2)}, u32[]{:S(2)}) collective-permute-start(bf16[128,1024]{1,0:T(8,128)(2,1)S(1)} %get-tuple-element.241), channel_id=1, source_target_pairs={{0,4},{4,8},{8,12},{12,16},{16,20},{20,24},{24,28},{28,32},{32,36}... | collective-permute-start | bytes 786440 | tf_op jit(solution)/shard_map/ppermute | solution.py:17
  12.9 38.2 %collective-permute-start.1 = (bf16[128,1024]{1,0:T(8,128)(2,1)S(1)}, bf16[128,1024]{1,0:T(8,128)(2,1)S(1)}, u32[]{:S(2)}, u32[]{:S(2)}) collective-permute-start(bf16[128,1024]{1,0:T(8,128)(2,1)S(1)} %get-tuple-element.242), channel_id=1, source_target_pairs={{4,0},{8,4},{12,8},{16,12},{20,16},{24,20},{28,24},{32,28},{36,32}... | collective-permute-start | bytes 786440 | tf_op jit(solution)/shard_map/ppermute | solution.py:19
  41.9 3.4 slice-start
  68.2 6.3 %copy-start.6 = (f32[2,128,1024]{1,2,0:T(8,128)S(1)}, f32[2,128,1024]{1,2,0:T(8,128)}, u32[]{:S(2)}) copy-start(f32[2,128,1024]{1,2,0:T(8,128)} %get-tuple-element.318) | copy-start | bytes 3145732 | tf_op jit(solution)/shard_map/while
  74.6 1.3 copy-start.7
  84.4 18.8 %copy-start.3 = (f32[64,128]{1,0:T(8,128)S(1)}, f32[64,128]{1,0:T(8,128)}, u32[]{:S(2)}) copy-start(f32[64,128]{1,0:T(8,128)} %get-tuple-element.316) | copy-start | bytes 98308 | tf_op jit(solution)/shard_map/while
  103.2 0.6 copy-start.4
  113.5 6.3 %copy-start.6 = (f32[2,128,1024]{1,2,0:T(8,128)S(1)}, f32[2,128,1024]{1,2,0:T(8,128)}, u32[]{:S(2)}) copy-start(f32[2,128,1024]{1,2,0:T(8,128)} %get-tuple-element.318) | copy-start | bytes 3145732 | tf_op jit(solution)/shard_map/while
  119.8 1.3 copy-start.7
  129.6 18.8 %copy-start.3 = (f32[64,128]{1,0:T(8,128)S(1)}, f32[64,128]{1,0:T(8,128)}, u32[]{:S(2)}) copy-start(f32[64,128]{1,0:T(8,128)} %get-tuple-element.316) | copy-start | bytes 98308 | tf_op jit(solution)/shard_map/while
  148.4 0.6 copy-start.4
  161.5 0.6 copy-start.9
  161.5 0.6 copy-start.8
  161.5 3.6 copy-start.5
  162.3 188.0 %collective-permute-start.2 = (bf16[128,1024]{1,0:T(8,128)(2,1)S(1)}, bf16[128,1024]{1,0:T(8,128)(2,1)S(1)}, u32[]{:S(2)}, u32[]{:S(2)}) collective-permute-start(bf16[128,1024]{1,0:T(8,128)(2,1)S(1)} %slice.80), channel_id=1, source_target_pairs={{4,0},{8,4},{12,8},{16,12},{20,16},{24,20},{28,24},{32,28},{36,32}... | collective-permute-start | bytes 786440 | tf_op jit(solution)/shard_map/ppermute | solution.py:19
  350.5 19.1 %collective-permute-start.3 = (bf16[128,1024]{1,0:T(8,128)(2,1)S(1)}, bf16[128,1024]{1,0:T(8,128)(2,1)S(1)}, u32[]{:S(2)}, u32[]{:S(2)}) collective-permute-start(bf16[128,1024]{1,0:T(8,128)(2,1)S(1)} %get-tuple-element.240), channel_id=1, source_target_pairs={{0,4},{4,8},{8,12},{12,16},{16,20},{20,24},{24,28},{28,32},{32,36}... | collective-permute-start | bytes 786440 | tf_op jit(solution)/shard_map/ppermute | solution.py:17
  358.7 19.4 %copy-start = (bf16[3,256,1024]{2,1,0:T(8,128)(2,1)S(1)}, bf16[3,256,1024]{2,1,0:T(8,128)(2,1)}, u32[]{:S(2)}) copy-start(bf16[3,256,1024]{2,1,0:T(8,128)(2,1)} %param.7) | copy-start | bytes 4718596
  369.7 5.6 %copy-start.2 = (f32[128,64,16]{0,2,1:T(8,128)S(1)}, f32[128,64,16]{0,2,1:T(8,128)}, u32[]{:S(2)}) copy-start(f32[128,64,16]{0,2,1:T(8,128)} %slice.81) | copy-start | bytes 1572868
  369.8 9.9 %copy-start.1 = (bf16[256,1024]{1,0:T(8,128)(2,1)S(1)}, bf16[256,1024]{1,0:T(8,128)(2,1)}, u32[]{:S(2)}) copy-start(bf16[256,1024]{1,0:T(8,128)(2,1)} %get-tuple-element.238) | copy-start | bytes 1572868
Sparse Core Ops, SparseCore 0:
  9.6 35.1 all-gather.1
  161.7 225.2 reduce-scatter.1
where the time goes:
time: 397 us; the launch traced here: 396 us
  blocking collectives  184 us (46%)
  local copies, waits for them, and re-layouts  83.6 us (21%)
  matrix products  54.2 us (14%)
  other arithmetic  21.3 us (5%)
  waiting for transfers between devices  17.7 us (4%)
  starting transfers between devices  16.4 us (4%)
  between operations  14.3 us (4%)
  loops' own time  3.97 us (1%)
    psum x1, blocking collectives, local(): grad_filters = lax.psum(filter_total, 'ctx') * grad_scale  184 us
    reshape x2, local copies, waits for them, and re-layouts, diagonals(): flattened.reshape(groups, tap_count, width + 1)[:, :, 1:tap_count + 1]  28.3 us
    dot_general x2, matrix products, advance(): jnp.einsum('gij,jgc->igc', kernel, window_f, precision=exact)  12.8 us
    reshape x1, local copies, waits for them, and re-layouts, banded(): jnp.broadcast_to(pattern[:, None, :], (groups, tap_count, width + 1))  12.3 us
    dot_general x2, matrix products, spread_back(): jnp.einsum('gij,igc->jgc', kernel, grad_f, precision=lax.Precision.HIGHEST)  11 us
    ppermute x2, starting transfers between devices, extended_2(): lax.ppermute(head, axis, [((i + 1) % count, i) for i in range(ends)])  10.9 us
    ppermute x2, waiting for transfers between devices, extended_2(): lax.ppermute(tail, axis, [(i, (i + 1) % count) for i in range(ends)])  10.9 us
    dot_general x2, matrix products, advance(): jnp.einsum('gij,igc->jgc', kernel, grad_f, precision=exact)  10.7 us
  transfers between devices with their start and end apart: 6, of which 2 were waited for; matrix products, arithmetic and copies ran while one was open for 12% of the time, Pallas kernels for 0%

commit v1 on v0

v1 whole, which is shorter than its diff:
```python
import functools
import math

import jax
import jax.numpy as jnp
from jax import lax
from jax.experimental import pallas as pl
from jax.experimental.pallas import tpu as pltpu
from jax.sharding import PartitionSpec as P

LANES = 128
TAPS = 128
GW = 16
PER = LANES // GW


def doc_reach(positions, doc_lens):
    starts = jnp.cumsum(doc_lens) - doc_lens
    below = jnp.where(starts[None, :] <= positions[:, None], starts[None, :], 0)
    return positions - jnp.max(below, axis=1)


def grid_ids():
    rows = lax.broadcasted_iota(jnp.int32, (TAPS, TAPS), 0)
    cols = lax.broadcasted_iota(jnp.int32, (TAPS, TAPS), 1)
    return rows, cols


def sheared(row):
    return pltpu.roll(jnp.broadcast_to(row, (TAPS, TAPS)), 0, 1, stride=1, stride_axis=0)


def window_masks(reach, turned=False):
    rows, cols = grid_ids()
    if turned:
        rows = TAPS - 1 - rows
    prev = (rows < cols) & (rows - cols + TAPS <= reach)
    own = (rows >= cols) & (rows - cols <= reach)
    return prev, own


def conv_tile(h_ref, halo_ref, frev_ref, ocol_ref, q_ref, c_ref, y_ref, stack_ref):
    group = lax.broadcasted_iota(jnp.int32, (TAPS, LANES), 1) // GW
    masks = [window_masks(ocol_ref[a * TAPS : (a + 1) * TAPS, :]) for a in range(2)]
    for g in range(PER):
        circ = sheared(frev_ref[g : g + 1, :])
        for a in range(2):
            prev, own = masks[a]
            rows = slice(g * TAPS, (g + 1) * TAPS)
            stack_ref[a, rows, :TAPS] = jnp.where(prev, circ, 0.0).astype(jnp.bfloat16)
            stack_ref[a, rows, TAPS:] = jnp.where(own, circ, 0.0).astype(jnp.bfloat16)
    for a in range(2):
        span = slice(a * TAPS, (a + 1) * TAPS)
        window = jnp.concatenate([halo_ref[span, :], h_ref[span, :]], axis=0)
        out = jnp.dot(stack_ref[a], window, preferred_element_type=jnp.float32)
        c = out[:TAPS]
        for g in range(1, PER):
            c = jnp.where(group == g, out[g * TAPS : (g + 1) * TAPS], c)
        c_ref[span, :] = c
        y_ref[span, :] = (q_ref[0, span, :].astype(jnp.float32) * c).astype(jnp.bfloat16)


def back_tile(
    kv_ref, h_ref, halo_ref, dc_ref, next_ref, dy_ref, c_ref, f_ref, ocol_ref, orow_ref,
    out_ref, gf_ref, stack_ref, mask_ref,
):
    group = lax.broadcasted_iota(jnp.int32, (TAPS, LANES), 1) // GW
    rows, cols = grid_ids()
    spread = []
    for a in range(2):
        mine = orow_ref[a : a + 1, :]
        following = orow_ref[2 + a : 3 + a, :]
        own = (cols >= rows) & (cols - rows <= mine)
        prev = (cols < rows) & (cols - rows + TAPS <= following)
        spread.append((own, prev))
    for g in range(PER):
        circ = sheared(f_ref[g : g + 1, :])
        for a in range(2):
            own, prev = spread[a]
            part = slice(g * TAPS, (g + 1) * TAPS)
            stack_ref[a, part, :TAPS] = jnp.where(own, circ, 0.0).astype(jnp.bfloat16)
            stack_ref[a, part, TAPS:] = jnp.where(prev, circ, 0.0).astype(jnp.bfloat16)
    turn = jnp.where(rows + cols == TAPS - 1, 1.0, 0.0).astype(jnp.bfloat16)
    for a in range(2):
        span = slice(a * TAPS, (a + 1) * TAPS)
        pair = jnp.concatenate([dc_ref[span, :], next_ref[span, :]], axis=0)
        out = jnp.dot(stack_ref[a], pair, preferred_element_type=jnp.float32)
        dh = out[:TAPS]
        for g in range(1, PER):
            dh = jnp.where(group == g, out[g * TAPS : (g + 1) * TAPS], dh)
        out_ref[0, span, :] = (dy_ref[span, :] * c_ref[span, :]).astype(jnp.bfloat16)
        out_ref[1, span, :] = (dh * kv_ref[1, span, :].astype(jnp.float32)).astype(jnp.bfloat16)
        out_ref[2, span, :] = (dh * kv_ref[0, span, :].astype(jnp.float32)).astype(jnp.bfloat16)
        dc = jnp.dot(turn, dc_ref[span, :], preferred_element_type=jnp.float32)
        for g in range(PER):
            mask_ref[a, g * TAPS : (g + 1) * TAPS, :] = jnp.where(group == g, dc, 0.0).astype(
                jnp.bfloat16
            )
    products = []
    for a in range(2):
        span = slice(a * TAPS, (a + 1) * TAPS)
        window = jnp.concatenate([halo_ref[span, :], h_ref[span, :]], axis=0)
        products.append(
            lax.dot_general(
                mask_ref[a], window, (((1,), (1,)), ((), ())), preferred_element_type=jnp.float32
            )
        )
    masks = [window_masks(ocol_ref[(2 + a) * TAPS : (3 + a) * TAPS, :], True) for a in range(2)]
    for g in range(PER):
        part = slice(g * TAPS, (g + 1) * TAPS)
        total = jnp.zeros((TAPS, TAPS), jnp.float32)
        for a in range(2):
            prev, own = masks[a]
            total = total + jnp.where(prev, products[a][part, :TAPS], 0.0)
            total = total + jnp.where(own, products[a][part, TAPS:], 0.0)
        lined = pltpu.roll(total, 1, 1, stride=1, stride_axis=0)
        gf_ref[g : g + 1, :] = jnp.sum(lined, axis=0, keepdims=True)


def lane_tile(rows):
    return pl.BlockSpec((rows, LANES), lambda i: (0, i))


def whole(shape):
    return pl.BlockSpec(shape, lambda i: tuple(0 for _ in shape))


def convolve(h, halo, frev, ocol, qkv):
    rows, width = h.shape
    return pl.pallas_call(
        conv_tile,
        grid=(width // LANES,),
        in_specs=[
            lane_tile(rows), lane_tile(rows),
            pl.BlockSpec((PER, TAPS), lambda i: (i, 0)),
            whole(ocol.shape),
            pl.BlockSpec((1, rows, LANES), lambda i: (0, 0, i)),
        ],
        out_specs=[lane_tile(rows), lane_tile(rows)],
        out_shape=[
            jax.ShapeDtypeStruct((rows, width), jnp.float32),
            jax.ShapeDtypeStruct((rows, width), jnp.bfloat16),
        ],
        scratch_shapes=[pltpu.VMEM((2, PER * TAPS, 2 * TAPS), jnp.bfloat16)],
        cost_estimate=pl.CostEstimate(
            flops=2 * 2 * PER * TAPS * 2 * TAPS * LANES * 8, bytes_accessed=4 << 20, transcendentals=0
        ),
    )(h, halo, frev, ocol, qkv)


def pull_back(qkv, h, halo, dc, following, dy, c, filt, ocol, orow):
    rows, width = h.shape
    return pl.pallas_call(
        back_tile_from,
        grid=(width // LANES,),
        in_specs=[
            pl.BlockSpec((1, rows, LANES), lambda i: (1, 0, i)),
            pl.BlockSpec((1, rows, LANES), lambda i: (2, 0, i)),
            lane_tile(rows), lane_tile(rows), lane_tile(rows), lane_tile(rows),
            lane_tile(rows), lane_tile(rows),
            pl.BlockSpec((PER, TAPS), lambda i: (i, 0)),
            whole(ocol.shape), whole(orow.shape),
        ],
        out_specs=[
            pl.BlockSpec((3, rows, LANES), lambda i: (0, 0, i)),
            pl.BlockSpec((PER, TAPS), lambda i: (i, 0)),
        ],
        out_shape=[
            jax.ShapeDtypeStruct((3, rows, width), jnp.bfloat16),
            jax.ShapeDtypeStruct((width // GW, TAPS), jnp.float32),
        ],
        scratch_shapes=[
            pltpu.VMEM((2, PER * TAPS, 2 * TAPS), jnp.bfloat16),
            pltpu.VMEM((2, PER * TAPS, LANES), jnp.bfloat16),
        ],
        cost_estimate=pl.CostEstimate(
            flops=4 * 2 * PER * TAPS * 2 * TAPS * LANES * 8, bytes_accessed=8 << 20, transcendentals=0
        ),
    )(qkv, qkv, h, halo, dc, following, dy, c, filt, ocol, orow)


class Pair:
    def __init__(self, first, second):
        self.parts = (first, second)

    def __getitem__(self, key):
        return self.parts[key[0]][(0,) + key[1:]]


def back_tile_from(k_ref, v_ref, *refs):
    back_tile(Pair(k_ref, v_ref), *refs)


def shift(cells, up):
    count = lax.axis_size("ctx")
    pairs = [(i, i + 1) if up else (i + 1, i) for i in range(count - 1)]
    return lax.ppermute(cells, "ctx", pairs)


def local(qkv, filters, w_out, cotangent, doc_lens):
    tok_ctx, width = qkv.shape[1:]
    n_ctx = lax.axis_size("ctx")
    rank = lax.axis_index("ctx")
    last = rank == n_ctx - 1
    tokens = tok_ctx * n_ctx
    full_cot = lax.all_gather(cotangent, "tp", axis=0, tiled=True)
    queries = qkv[0]
    hidden = (qkv[1].astype(jnp.float32) * qkv[2].astype(jnp.float32)).astype(jnp.bfloat16)
    tail_first = shift(hidden[:TAPS], True)
    tail_second = jnp.where(last, hidden[:TAPS], shift(hidden[TAPS:], False))
    halo = jnp.concatenate([tail_first, tail_second], axis=0)
    ids = jnp.arange(TAPS, dtype=jnp.int32)
    starts = jnp.stack([rank, 2 * n_ctx - 1 - rank, rank + 1, 2 * n_ctx - rank]) * TAPS
    reach = doc_reach((starts[:, None] + ids[None, :]).reshape(4 * TAPS), doc_lens)
    orow = reach.reshape(4, TAPS)
    ocol = jnp.concatenate([orow[:2], jnp.flip(orow[:2], axis=1)], axis=0).reshape(4 * TAPS, 1)
    filt = filters.astype(jnp.float32)
    frev = jnp.concatenate([filt[:, :1], jnp.flip(filt[:, 1:], axis=1)], axis=1)
    c, y = convolve(hidden, halo, frev, ocol, qkv)
    scale = 1.0 / math.sqrt(tokens)
    partial = lax.dot_general(
        full_cot, y, (((0,), (0,)), ((), ())), preferred_element_type=jnp.float32
    )
    grad_w = lax.psum_scatter(partial, "ctx", scatter_dimension=0, tiled=True) * scale
    grad_y = jnp.dot(full_cot, w_out, preferred_element_type=jnp.float32)
    grad_c = (queries.astype(jnp.float32) * grad_y).astype(jnp.bfloat16)
    head_first = jnp.where(last, grad_c[TAPS:], shift(grad_c[:TAPS], False))
    head_second = shift(grad_c[TAPS:], True)
    following = jnp.concatenate([head_first, head_second], axis=0)
    grad_qkv, gf = pull_back(qkv, hidden, halo, grad_c, following, grad_y, c, filt, ocol, orow)
    gf = lax.psum(gf, "ctx")
    gf = jnp.concatenate([gf[:, :1], jnp.flip(gf[:, 1:], axis=1)], axis=1) * scale
    return (grad_qkv, gf, grad_w)


def solution(mesh):
    return jax.shard_map(
        local,
        mesh=mesh,
        in_specs=(P(None, "ctx", "tp"), P("tp", None), P(None, "tp"), P(("ctx", "tp"), None), P()),
        out_specs=(P(None, "ctx", "tp"), P("tp", None), P("ctx", "tp")),
        check_vma=False,
    )
```

time: 397 us -> 301 us (0.76)
  local copies, waits for them, and re-layouts: 83.6 us -> 4 us
  matrix products: 54.2 us -> 16.6 us
  waiting for transfers between devices: 17.7 us -> 42.9 us
  Pallas kernels: 0 us -> 18.7 us
  other arithmetic: 21.3 us -> 7.8 us
  blocking collectives: 184 us -> 177 us
  loops' own time: 3.97 us -> 0 us
    reshape x3 -> x1, local copies, waits for them, and re-layouts: 40.6 us -> 0.87 us  [local(): jnp.concatenate([orow[:2], jnp.flip(orow[:2], axis=1)], axis=0)]
    dot_general x9 -> x1, matrix products: 46.9 us -> 9.88 us  [local(): lax.dot_general(full_cot, y, (((0,), (0,)), ((), ())), preferred_element_...]
    ppermute x4, waiting for transfers between devices: 10.9 us -> 37.3 us  [shift(): return lax.ppermute(cells, 'ctx', pairs)]
    pallas_call x0 -> x2, Pallas kernels: none -> 18.7 us  [the longest x1 11 us: pull_back(): pl.pallas_call(back_tile_from, grid=(width // LANES,), in_specs=[pl.Block...]
    while x18 -> x0, local copies, waits for them, and re-layouts: 10.7 us -> none
    reduce_sum x2 -> x0, other arithmetic: 9.07 us -> none  [diagonals(): return jnp.flip(jnp.sum(sheared, axis=1), axis=1)]
    pad x2 -> x0, local copies, waits for them, and re-layouts: 7.5 us -> none  [diagonals(): jnp.pad(products.reshape(groups, tap_count * width), ((0, 0), (0, tap_cou...]
    psum x1, blocking collectives: 184 us -> 177 us  [local(): gf = lax.psum(gf, 'ctx')]
  transfers between devices with their start and end apart: 6 -> 6, of which waited for: 2 -> 4; matrix products, arithmetic and copies ran while one was open for 12% -> 5% of each run, Pallas kernels for 0% -> 6%
where the time goes in v1:
time: 301 us
  blocking collectives  177 us (59%)
  waiting for transfers between devices  42.9 us (14%)
  starting transfers between devices  18.8 us (6%)
  Pallas kernels  18.7 us (6%)
  matrix products  16.6 us (6%)
  between operations  14.2 us (5%)
  other arithmetic  7.8 us (3%)
  local copies, waits for them, and re-layouts  4 us (1%)
    psum x1, blocking collectives, local(): gf = lax.psum(gf, 'ctx')  177 us
    ppermute x4, waiting for transfers between devices, shift(): return lax.ppermute(cells, 'ctx', pairs)  37.3 us
    ppermute x4, starting transfers between devices, shift(): return lax.ppermute(cells, 'ctx', pairs)  18.7 us
    pallas_call x1, Pallas kernels, pull_back(): pl.pallas_call(back_tile_from, grid=(width // LANES,), in_specs=[pl.Block...  11 us
    dot_general x1, matrix products, local(): lax.dot_general(full_cot, y, (((0,), (0,)), ((), ())), preferred_element_...  9.88 us
    pallas_call x1, Pallas kernels, convolve(): pl.pallas_call(conv_tile, grid=(width // LANES,), in_specs=[lane_tile(row...  7.71 us
    dot_general x1, matrix products, local(): grad_y = jnp.dot(full_cot, w_out, preferred_element_type=jnp.float32)  6.74 us
  transfers between devices with their start and end apart: 6, of which 4 were waited for; matrix products, arithmetic and copies ran while one was open for 5% of the time, Pallas kernels for 6%

profile of v1, /device:TPU:4, one launch (start us, length us, event | category | flops | bytes accessed | tf_op | source)
XLA Modules:
  0.0 300.5 jit_solution(12288462545195658528)
XLA Ops:
  7.2 0.7 all-gather.2.cloned.1.call-update
  8.0 1.4 multiply_convert_fusion
  9.4 3.5 %collective-permute-start = (bf16[128,1024]{1,0:T(8,128)(2,1)S(1)}, bf16[128,1024]{1,0:T(8,128)(2,1)S(1)}, u32[]{:S(2)}, u32[]{:S(2)}) collective-permute-start(bf16[128,1024]{1,0:T(8,128)(2,1)S(1)} %get-tuple-element.22), channel_id=1, source_target_pairs={{0,4},{4,8},{8,12},{12,16},{16,20},{20,24},{24,28},{28,32},{32,36}... | collective-permute-start | bytes 786440 | tf_op jit(solution)/shard_map/ppermute | solution.py:197
  12.9 8.1 %collective-permute-start.1 = (bf16[128,1024]{1,0:T(8,128)(2,1)S(1)}, bf16[128,1024]{1,0:T(8,128)(2,1)S(1)}, u32[]{:S(2)}, u32[]{:S(2)}) collective-permute-start(bf16[128,1024]{1,0:T(8,128)(2,1)S(1)} %get-tuple-element.23), channel_id=1, source_target_pairs={{4,0},{8,4},{12,8},{16,12},{20,16},{24,20},{28,24},{32,28},{36,32}... | collective-permute-start | bytes 786440 | tf_op jit(solution)/shard_map/ppermute | solution.py:197
  21.0 0.1 copy.16
  21.1 0.1 reduce-window.9
  21.2 0.1 reduce
  21.3 0.1 add_multiply_fusion
  21.5 0.1 select_reduce_fusion
  21.6 1.0 fusion.6.h_ref.refs_0_
  22.8 0.1 rev.12
  22.9 0.7 pad_maximum_fusion.2.frev_ref
  23.6 0.9 copy.17.ocol_ref.refs_7_
  24.5 6.8 %collective-permute-done.1 = bf16[128,1024]{1,0:T(8,128)(2,1)S(1)} collective-permute-done((bf16[128,1024]{1,0:T(8,128)(2,1)S(1)}, bf16[128,1024]{1,0:T(8,128)(2,1)S(1)}, u32[]{:S(2)}, u32[]{:S(2)}) %collective-permute-start.1) | collective-permute-done | bytes 262176 | tf_op jit(solution)/shard_map/ppermute | solution.py:197
  31.4 0.8 pad_maximum_fusion.halo_ref.refs_1_
  32.2 7.7 %shard_map.76 = (f32[256,1024]{1,0:T(8,128)}, bf16[256,1024]{1,0:T(8,128)(2,1)}) custom-call(bf16[256,1024]{1,0:T(8,128)(2,1)} %fusion.6.h_ref.refs_0_, bf16[256,1024]{1,0:T(8,128)(2,1)} %pad_maximum_fusion.halo_ref.refs_1_, f32[64,128]{1,0:T(8,128)} %pad_maximum_fusion.2.frev_ref, s32[512,1]{1,0:T(8,128)} %copy.17.ocol_ref.refs_7_, bf16[3,256,1024]{2,1,0:T(8,128)(2,1)} %v_ref.1), custom_call_target="tpu_custom_call" | custom-call | flops 1073741824 | bytes 4194304 | tf_op jit(solution)/shard_map/pallas_call | solution.py:130
  39.9 4.9 %all-gather.2.cloned.1.call-done = bf16[256,4096]{1,0:T(8,128)(2,1)} async-done(((bf16[64,4096]{1,0:T(8,128)(2,1)}), bf16[256,4096]{1,0:T(8,128)(2,1)}) %all-gather.2.cloned.1.call-update) | async-done | bytes 2097168 | tf_op jit(solution)/shard_map/all_gather | solution.py:206
  44.8 9.9 %convolution_bitcast_fusion = f32[4096,1024]{0,1:T(8,128)} fusion(bf16[256,1024]{1,0:T(8,128)(2,1)} %get-tuple-element.10, bf16[256,4096]{1,0:T(8,128)(2,1)} %all-gather.2.cloned.1.call-done), kind=kOutput, calls=%fused_computation | convolution fusion | flops 2147483648 | bytes 19398656 | tf_op jit(solution)/shard_map/dot_general | solution.py:221
  54.8 1.6 copy-done.1
  56.3 6.7 %fusion = (bf16[256,1024]{1,0:T(8,128)(2,1)S(1)}, f32[256,1024]{1,0:T(8,128)}) fusion(bf16[3,256,1024]{2,1,0:T(8,128)(2,1)} %v_ref.1, bf16[256,4096]{1,0:T(8,128)(2,1)S(1)} %copy-done.1, bf16[4096,1024]{1,0:T(8,128)(2,1)} %param.7), kind=kOutput, calls=%fused_computation.2 | convolution fusion | flops 2148270080 | bytes 12582912 | tf_op jit(solution)/shard_map/dot_general | solution.py:225
  63.1 5.2 %collective-permute-start.2 = (bf16[128,1024]{1,0:T(8,128)(2,1)S(1)}, bf16[128,1024]{1,0:T(8,128)(2,1)S(1)}, u32[]{:S(2)}, u32[]{:S(2)}) collective-permute-start(bf16[128,1024]{1,0:T(8,128)(2,1)S(1)} %slice.64), channel_id=1, source_target_pairs={{4,0},{8,4},{12,8},{16,12},{20,16},{24,20},{28,24},{32,28},{36,32}... | collective-permute-start | bytes 786440 | tf_op jit(solution)/shard_map/ppermute | solution.py:197
  68.3 11.2 %collective-permute-done.2 = bf16[128,1024]{1,0:T(8,128)(2,1)S(1)} collective-permute-done((bf16[128,1024]{1,0:T(8,128)(2,1)S(1)}, bf16[128,1024]{1,0:T(8,128)(2,1)S(1)}, u32[]{:S(2)}, u32[]{:S(2)}) %collective-permute-start.2) | collective-permute-done | bytes 262176 | tf_op jit(solution)/shard_map/ppermute | solution.py:197
  79.6 1.9 collective-permute-start.3
  81.5 0.6 convert_element_type.32.refs_6_
  82.1 19.2 %collective-permute-done.3 = bf16[128,1024]{1,0:T(8,128)(2,1)S(1)} collective-permute-done((bf16[128,1024]{1,0:T(8,128)(2,1)S(1)}, bf16[128,1024]{1,0:T(8,128)(2,1)S(1)}, u32[]{:S(2)}, u32[]{:S(2)}) %collective-permute-start.3) | collective-permute-done | bytes 262176 | tf_op jit(solution)/shard_map/ppermute | solution.py:197
  101.4 0.8 pad_maximum_fusion.1.refs_3_
  102.2 11.0 %shard_map.77 = (bf16[3,256,1024]{2,1,0:T(8,128)(2,1)}, f32[64,128]{1,0:T(8,128)}) custom-call(bf16[3,256,1024]{2,1,0:T(8,128)(2,1)} %v_ref.1, bf16[3,256,1024]{2,1,0:T(8,128)(2,1)} %v_ref.1, bf16[256,1024]{1,0:T(8,128)(2,1)} %fusion.6.h_ref.refs_0_, bf16[256,1024]{1,0:T(8,128)(2,1)} %pad_maximum_fusion.halo_ref.refs_1_, bf16[256,1024]{1,0:T(8,128)(2,1)} %copy-done.2, ...), custom_call_target="tpu_custom_call" | custom-call | flops 2147483648 | bytes 8388608 | tf_op jit(solution)/shard_map/pallas_call | solution.py:153
  113.2 177.5 %psum.7 = f32[64,128]{1,0:T(8,128)S(1)} all-reduce(f32[64,128]{1,0:T(8,128)} %get-tuple-element.9), channel_id=1, replica_groups=mesh['ctx'=32,'tp'=4] {'ctx'}, use_global_device_ids=true, to_apply=%region_2.3 | all-reduce | flops 8192 | bytes 65536 | tf_op jit(solution)/shard_map/psum | solution.py:231
  290.7 0.1 slice.68
  290.9 0.7 maximum_multiply_fusion
  291.6 1.1 broadcast_multiply_fusion
  292.7 1.0 copy.19
  (29 shorter events, 0.7 us)
Async XLA Ops:
  7.2 14.4 %copy-start = (bf16[3,256,1024]{2,1,0:T(8,128)(2,1)S(1)}, bf16[3,256,1024]{2,1,0:T(8,128)(2,1)}, u32[]{:S(2)}) copy-start(bf16[3,256,1024]{2,1,0:T(8,128)(2,1)} %v_ref.1) | copy-start | bytes 4718596
  7.2 13.8 %copy-start.5 = (s32[64]{0:T(128)S(1)}, s32[64]{0:T(128)}, u32[]{:S(2)}) copy-start(s32[64]{0:T(128)} %param.9) | copy-start | bytes 772
  7.2 37.7 %all-gather.2.cloned.1.call-start = ((), (), s32[]{:S(2)}) async-start(), calls=%async_computation.1 | async-start | bytes 2621440 | tf_op jit(solution)/shard_map/all_gather | solution.py:206
  7.9 14.7 %copy-start.3 = (bf16[64,128]{1,0:T(8,128)(2,1)S(1)}, bf16[64,128]{1,0:T(8,128)(2,1)}, u32[]{:S(2)}) copy-start(bf16[64,128]{1,0:T(8,128)(2,1)} %param.6) | copy-start | bytes 49156
  7.9 283.6 %reduce-scatter.2.cloned.1.call-start = ((), (), s32[]{:S(2)}) async-start(), calls=%async_computation.2 | async-start | bytes 17301504 | tf_op jit(solution)/shard_map/reduce_scatter | solution.py:224
  9.4 21.9 %collective-permute-start = (bf16[128,1024]{1,0:T(8,128)(2,1)S(1)}, bf16[128,1024]{1,0:T(8,128)(2,1)S(1)}, u32[]{:S(2)}, u32[]{:S(2)}) collective-permute-start(bf16[128,1024]{1,0:T(8,128)(2,1)S(1)} %get-tuple-element.22), channel_id=1, source_target_pairs={{0,4},{4,8},{8,12},{12,16},{16,20},{20,24},{24,28},{28,32},{32,36}... | collective-permute-start | bytes 786440 | tf_op jit(solution)/shard_map/ppermute | solution.py:197
  12.9 18.4 %collective-permute-start.1 = (bf16[128,1024]{1,0:T(8,128)(2,1)S(1)}, bf16[128,1024]{1,0:T(8,128)(2,1)S(1)}, u32[]{:S(2)}, u32[]{:S(2)}) collective-permute-start(bf16[128,1024]{1,0:T(8,128)(2,1)S(1)} %get-tuple-element.23), channel_id=1, source_target_pairs={{4,0},{8,4},{12,8},{16,12},{20,16},{24,20},{28,24},{32,28},{36,32}... | collective-permute-start | bytes 786440 | tf_op jit(solution)/shard_map/ppermute | solution.py:197
  22.7 17.2 %copy-start.4 = (s32[4,128]{1,0:T(4,128)}, s32[4,128]{1,0:T(4,128)S(1)}, u32[]{:S(2)}) copy-start(s32[4,128]{1,0:T(4,128)S(1)} %bitcast_subtract_fusion.refs_8_) | copy-start | bytes 6148
  54.7 1.6 copy-start.1
  63.1 39.1 %copy-start.2 = (bf16[256,1024]{1,0:T(8,128)(2,1)}, bf16[256,1024]{1,0:T(8,128)(2,1)S(1)}, u32[]{:S(2)}) copy-start(bf16[256,1024]{1,0:T(8,128)(2,1)S(1)} %get-tuple-element.24.refs_2_) | copy-start | bytes 1572868
  63.1 16.4 %collective-permute-start.2 = (bf16[128,1024]{1,0:T(8,128)(2,1)S(1)}, bf16[128,1024]{1,0:T(8,128)(2,1)S(1)}, u32[]{:S(2)}, u32[]{:S(2)}) collective-permute-start(bf16[128,1024]{1,0:T(8,128)(2,1)S(1)} %slice.64), channel_id=1, source_target_pairs={{4,0},{8,4},{12,8},{16,12},{20,16},{24,20},{28,24},{32,28},{36,32}... | collective-permute-start | bytes 786440 | tf_op jit(solution)/shard_map/ppermute | solution.py:197
  79.6 21.8 %collective-permute-start.3 = (bf16[128,1024]{1,0:T(8,128)(2,1)S(1)}, bf16[128,1024]{1,0:T(8,128)(2,1)S(1)}, u32[]{:S(2)}, u32[]{:S(2)}) collective-permute-start(bf16[128,1024]{1,0:T(8,128)(2,1)S(1)} %get-tuple-element.21), channel_id=1, source_target_pairs={{0,4},{4,8},{8,12},{12,16},{16,20},{20,24},{24,28},{28,32},{32,36}... | collective-permute-start | bytes 786440 | tf_op jit(solution)/shard_map/ppermute | solution.py:197
Sparse Core Ops, SparseCore 0:
  9.7 35.1 all-gather.1
  54.9 229.6 reduce-scatter.1
